TPU v7x, 256 devices: a whole 4x4x8 slice. The times are simulated.
256 devices in a mesh: curve: 128 (over y, z, x_lo, core), chan: 2 (over x_hi).
Axes of the slice: x: 4 (x_hi: 2, x_lo: 2; x = x_hi * 2 + x_lo), y: 4, z: 8, core: 2. Of those that a mesh axis runs over, the one named last changes fastest.
Arguments:
- features: bfloat16 [524288, 256], P('curve', 'chan'), may hold values from -6 to 6
- cotangent: bfloat16 [524288, 256], P('curve', 'chan'), may hold values from -6 to 6
- near_kernel: bfloat16 [4096, 8, 128, 128], P('curve'), may hold values from -0.1875 to 0.1875
- near_index: int32 [4096, 8], P('curve'), may hold values from 0 to 4095, as said below
- near_count: int32 [4096], P('curve'), may hold values from 1 to 8, as said below
- basis_in: bfloat16 [4096, 16, 128], P('curve'), may hold values from -0.09375 to 0.09375
- basis_out: bfloat16 [4096, 128, 16], P('curve'), may hold values from -1.5 to 1.5
- far_kernel: float32 [128, 8, 16, 16], P('curve'), may hold values from -0.5 to 0.5
- far_index: int32 [128, 8], P('curve'), may hold values from 0 to 127, as said below
- channel_mix: float32 [256, 256], replicated, may hold values from -0.375 to 0.375
Outputs:
- layer_out: bfloat16 [524288, 256], P('curve', 'chan')
- feature_grad: bfloat16 [524288, 256], P('curve', 'chan')
Inputs may be any that keep to these rules, and one draw needn't show every extreme that they name: `near_index`: slot 0 of block b holds b; every slot of block b holds a block from b - 32 to b. `near_count`: in every group of 32 blocks one block has all 8 slots live and another block has one. `far_index`: every partner of group g differs from g by 2 or more.
All inputs are finite; a program needn't handle non-finite values.
Results may differ from a plain program's by a relative error of at most 0.006.
Values may be sent and summed in bfloat16 or wider, within the bound.
No kernel may reach another device: no remote copies, remote signals or barrier semaphores. Data moves between devices by JAX's collectives and lax.ppermute only.
A program may use at most 128 MiB of HBM per device.

v0:
```python
import jax
import jax.numpy as jnp
from jax import lax
from jax.sharding import PartitionSpec as P


def shifted(value, axis, steps):
    count = lax.axis_size(axis)
    leading, last = (max(0, -steps), min(count, count - steps))
    return lax.ppermute(value, axis, [(source, source + steps) for source in range(leading, last)])


def split_up(value, dim, count):
    before, after = (value.shape[:dim], value.shape[dim + 1 :])
    return jnp.moveaxis(value.reshape(*before, count, -1, *after), dim, 0)


def sent_and_summed(value, axis, dim):
    blocks = split_up(value, dim, lax.axis_size(axis))
    arrived = lax.all_to_all(blocks, axis, split_axis=0, concat_axis=0, tiled=True)
    return arrived.sum(axis=0)


def body(
    features,
    cotangent,
    near_kernel,
    near_index,
    near_count,
    basis_in,
    basis_out,
    far_kernel,
    far_index,
    channel_mix,
):
    exact = lax.Precision.HIGHEST
    blocks, slots, panels, _ = near_kernel.shape
    width = features.shape[1]
    groups = lax.axis_size("curve")
    position = lax.axis_index("curve")
    chan_pos = lax.axis_index("chan")
    feat_blocks = features.reshape(blocks, panels, width)
    cot_blocks = cotangent.reshape(blocks, panels, width)
    live_slot = lax.iota(jnp.int32, slots)[None, :] < near_count[:, None]
    local_rows = near_index - (position * blocks - blocks)
    coarse = jnp.einsum(
        "brp,bpc->rc", basis_in, feat_blocks, preferred_element_type=jnp.float32
    ).astype(jnp.bfloat16)
    dfar = jnp.einsum("bpr,bpc->rc", basis_out, cot_blocks, preferred_element_type=jnp.float32)
    before = shifted(features, "curve", 1)
    extended = jnp.concatenate([before.reshape(blocks, panels, width), feat_blocks], axis=0)
    picked = extended[local_rows] * live_slot[:, :, None, None].astype(jnp.bfloat16)
    near = jnp.einsum("bspq,bsqc->bpc", near_kernel, picked, preferred_element_type=jnp.float32)
    mix_cols = lax.dynamic_slice_in_dim(channel_mix, chan_pos * width, width, 1)
    far_mats = far_kernel[0]
    partners = far_index[0]
    one_hot = (partners[:, None] == lax.iota(jnp.int32, groups)[None, :]).astype(jnp.float32)
    every = lax.all_gather(coarse[None], "curve", axis=0, tiled=True)
    chosen = jnp.einsum("ag,grc->arc", one_hot, every.astype(jnp.float32), precision=exact)
    partial_coef = jnp.einsum("aqr,arc->qc", far_mats, chosen, precision=exact)
    mix_rows = lax.dynamic_slice_in_dim(channel_mix, chan_pos * width, width, 0)
    term = jnp.dot(partial_coef, mix_rows, precision=exact, preferred_element_type=jnp.float32)
    far_coef = sent_and_summed(term, "chan", 1)
    far_low = far_coef.astype(jnp.bfloat16)
    layer = near + jnp.einsum("bpr,rc->bpc", basis_out, far_low, preferred_element_type=jnp.float32)
    layer_out = layer.astype(jnp.bfloat16).reshape(blocks * panels, width)
    contrib = jnp.einsum(
        "bspq,bpc->bsqc", near_kernel, cot_blocks, preferred_element_type=jnp.float32
    )
    slot_hot = (
        (local_rows[:, :, None] == lax.iota(jnp.int32, 2 * blocks)[None, None, :])
        & live_slot[:, :, None]
    ).astype(jnp.bfloat16)
    contrib_high = contrib.astype(jnp.bfloat16)
    contrib_low = (contrib - contrib_high.astype(jnp.float32)).astype(jnp.bfloat16)
    spread_near = jnp.einsum(
        "bse,bsqc->eqc", slot_hot, contrib_high, preferred_element_type=jnp.float32
    )
    spread_near = spread_near + jnp.einsum(
        "bse,bsqc->eqc", slot_hot, contrib_low, preferred_element_type=jnp.float32
    )
    arrived = shifted(spread_near[:blocks].astype(jnp.bfloat16), "curve", -1).astype(jnp.float32)
    nearback = spread_near[blocks:] + arrived
    unmix_term = jnp.dot(dfar, mix_cols.T, precision=exact, preferred_element_type=jnp.float32)
    dz_share = sent_and_summed(unmix_term, "chan", 1)
    spread = jnp.einsum("aqr,qc->arc", far_mats, dz_share, precision=exact)
    grad_terms = jnp.einsum("ag,arc->grc", one_hot, spread, precision=exact)
    dcoarse = lax.psum_scatter(grad_terms, "curve", scatter_dimension=0, tiled=True)[0]
    dcoarse_low = dcoarse.astype(jnp.bfloat16)
    grad = nearback + jnp.einsum(
        "brp,rc->bpc", basis_in, dcoarse_low, preferred_element_type=jnp.float32
    )
    feature_grad = grad.astype(jnp.bfloat16).reshape(blocks * panels, width)
    return (layer_out, feature_grad)


def solution(mesh):
    return jax.shard_map(
        body,
        mesh=mesh,
        in_specs=(
            P("curve", "chan"),
            P("curve", "chan"),
            P("curve", None, None, None),
            P("curve", None),
            P("curve"),
            P("curve", None, None),
            P("curve", None, None),
            P("curve", None, None, None),
            P("curve", None),
            P(),
        ),
        out_specs=(P("curve", "chan"), P("curve", "chan")),
        check_vma=False,
    )
```

profile of v0, /device:TPU:0, one launch (start us, length us, event | category | flops | bytes accessed | tf_op | source)
XLA Modules:
  0.0 787.8 jit_solution(6620656626656210797)
XLA Ops:
  7.2 0.7 iota_compare_fusion.2
  7.9 0.7 compare_select_fusion
  8.6 7.9 %subtract_convert_fusion = (bf16[32,8,128,128]{3,2,1,0:T(8,128)(2,1)}, bf16[32,8,128,128]{3,2,1,0:T(8,128)(2,1)S(1)}) fusion(bf16[32,8,128,128]{3,2,1,0:T(8,128)(2,1)} %param.12, bf16[32,128,128,1]{2,1,3,0:T(8,128)(2,1)S(1)} %bitcast.89), kind=kOutput, calls=%fused_computation.1 | convolution fusion | flops 1090519040 | bytes 26214400 | tf_op jit(solution)/shard_map/bspq,bpc->bsqc/dot_general | solution.py:67
  16.5 8.4 %fusion = f32[64,128,128,1]{2,0,3,1:T(8,128)S(1)} fusion(bf16[32,8,128,128]{3,2,1,0:T(8,128)(2,1)} %get-tuple-element.2, s32[32,8]{0,1:T(8,128)S(1)} %get-tuple-element.5, pred[32,8]{0,1:T(8,128)(4,1)S(1)} %get-tuple-element.6), kind=kOutput, calls=%fused_computation.2 | convolution fusion | flops 536903680 | bytes 12584192 | tf_op jit(solution)/shard_map/bse,bsqc->eqc/dot_general | solution.py:79
  25.1 5.5 bitcast_add_fusion
  30.5 2.0 copy-done.1
  32.5 1.2 slice.19
  33.7 1.3 collective-permute-start.1
  35.0 0.2 convolution_bitcast_fusion.3
  35.3 0.2 convolution_bitcast_fusion.1
  35.5 0.6 copy.55
  36.1 3.2 all-to-all-start.1
  39.4 4.0 collective-permute-start
  43.4 0.2 fusion.14
  43.7 164.0 %all-gather = bf16[2048,128]{1,0:T(8,128)(2,1)S(1)} all-gather(bf16[16,128]{1,0:T(8,128)(2,1)S(1)} %fusion.14), channel_id=2, replica_groups=mesh['curve'=128,'chan'=2] {'curve'}, dimensions={0}, use_global_device_ids=true | all-gather | bytes 528384 | tf_op jit(solution)/shard_map/all_gather | solution.py:58
  207.8 0.2 convolution_bitcast_fusion
  208.0 0.7 fusion.34
  208.7 1.6 copy.34
  210.3 0.2 fusion.15
  210.5 0.2 convolution_bitcast_fusion.4
  210.7 0.2 convolution_bitcast_fusion.2
  210.9 0.6 copy.56
  211.6 3.9 all-to-all-start
  215.7 1.3 copy.35
  217.0 3.9 all-to-all-done
  220.9 1.8 fusion.29
  222.7 1.7 pad_maximum_fusion
  224.4 8.5 %gather_fusion = bf16[256,128,128]{2,1,0:T(8,128)(2,1)} fusion(bf16[64,128,128]{2,1,0:T(8,128)(2,1)S(1)} %pad_maximum_fusion, s32[1024]{0:T(1024)S(1)} %pad_clamp_fusion), kind=kCustom, calls=%fused_computation | custom fusion | bytes 16778240 | tf_op jit(solution)/shard_map/gather | solution.py:52
  233.0 9.9 %fusion.11 = bf16[32,128,128]{2,1,0:T(8,128)(2,1)} fusion(f32[128,32,128]{0,2,1:T(8,128)} %fusion.29, bf16[32,8,128,128]{3,2,1,0:T(8,128)(2,1)} %param.12, bf16[32,8,128,128]{3,2,1,0:T(8,128)(2,1)} %bitcast.91, bf16[32,8]{1,0:T(8,128)(2,1)S(1)} %copy.25), kind=kOutput, calls=%fused_computation.16 | convolution fusion | flops 1091567616 | bytes 19923456 | tf_op jit(solution)/shard_map/bspq,bsqc->bpc/dot_general | solution.py:53
  242.8 534.3 %reduce-scatter.2.cloned.1.call-done = f32[1,16,128]{2,1,0:T(8,128)} async-done(((f32[128,16,128]{2,1,0:T(8,128)}), f32[1,16,128]{2,1,0:T(8,128)}) %reduce-scatter.2.cloned.1.call-update) | async-done | bytes 8208 | tf_op jit(solution)/shard_map/reduce_scatter | solution.py:88
  777.2 2.4 fusion.10
  779.6 1.4 copy.36
  (29 shorter events, 0.5 us)
Async XLA Ops:
  7.2 1.5 copy-start
  25.0 10.0 %copy-start.5 = (bf16[32,128,16]{1,2,0:T(8,128)(2,1)S(1)}, bf16[32,128,16]{1,2,0:T(8,128)(2,1)}, u32[]{:S(2)}) copy-start(bf16[32,128,16]{1,2,0:T(8,128)(2,1)} %param.16) | copy-start | bytes 393220
  25.0 10.3 %copy-start.6 = (f32[256,256]{1,0:T(8,128)S(1)}, f32[256,256]{1,0:T(8,128)}, u32[]{:S(2)}) copy-start(f32[256,256]{1,0:T(8,128)} %param.19) | copy-start | bytes 786436
  25.0 14.4 %copy-start.2 = (bf16[4096,128]{1,0:T(8,128)(2,1)S(1)}, bf16[4096,128]{1,0:T(8,128)(2,1)}, u32[]{:S(2)}) copy-start(bf16[4096,128]{1,0:T(8,128)(2,1)} %param.10) | copy-start | bytes 3145732
  25.0 18.4 %copy-start.4 = (bf16[32,16,128]{2,1,0:T(8,128)(2,1)S(1)}, bf16[32,16,128]{2,1,0:T(8,128)(2,1)}, u32[]{:S(2)}) copy-start(bf16[32,16,128]{2,1,0:T(8,128)(2,1)} %param.15) | copy-start | bytes 393220
  25.0 182.6 %copy-start.7 = (f32[1,8,16,16]{3,2,1,0:T(8,128)S(1)}, f32[1,8,16,16]{3,2,1,0:T(8,128)}, u32[]{:S(2)}) copy-start(f32[1,8,16,16]{3,2,1,0:T(8,128)} %param.17) | copy-start | bytes 24580
  25.0 182.9 %copy-start.8 = (s32[1,8]{1,0:T(1,128)S(1)}, s32[1,8]{1,0:T(1,128)}, u32[]{:S(2)}) copy-start(s32[1,8]{1,0:T(1,128)} %param.18) | copy-start | bytes 100
  30.5 2.0 copy-start.1
  33.7 209.1 %collective-permute-start.1 = (bf16[32,128,128]{2,0,1:T(8,128)(2,1)}, bf16[32,128,128]{2,0,1:T(8,128)(2,1)}, u32[]{:S(2)}, u32[]{:S(2)}) collective-permute-start(bf16[32,128,128]{2,0,1:T(8,128)(2,1)} %slice.19), channel_id=1, source_target_pairs={{2,0},{4,2},{6,4},{8,6},{10,8},{12,10},{14,12},{16,14},{18,16},{20... | collective-permute-start | bytes 3145736 | tf_op jit(solution)/shard_map/ppermute | solution.py:10
  36.1 171.6 %all-to-all-start.1 = ((f32[2,16,128]{2,1,0:T(8,128)}), f32[2,16,128]{2,1,0:T(8,128)S(1)}, u32[]{:S(2)}, u32[]{:S(2)}) async-start(f32[2,16,128]{2,1,0:T(8,128)} %bitcast.86), calls=%async_computation.1 | async-start | bytes 32768 | tf_op jit(solution)/shard_map/all_to_all | solution.py:20
  39.4 737.8 %reduce-scatter.2.cloned.1.call-start = ((), (), s32[]{:S(2)}) async-start(), calls=%async_computation.3 | async-start | bytes 1056768 | tf_op jit(solution)/shard_map/reduce_scatter | solution.py:88
  39.4 183.3 %collective-permute-start = (bf16[4096,128]{1,0:T(8,128)(2,1)S(1)}, bf16[4096,128]{1,0:T(8,128)(2,1)}, u32[]{:S(2)}, u32[]{:S(2)}) collective-permute-start(bf16[4096,128]{1,0:T(8,128)(2,1)S(1)} %copy-done.2), channel_id=1, source_target_pairs={{0,2},{2,4},{4,6},{6,8},{8,10},{10,12},{12,14},{14,16},{16,18},{18... | collective-permute-start | bytes 3145736 | tf_op jit(solution)/shard_map/ppermute | solution.py:10
  211.6 9.3 %all-to-all-start = ((f32[2,16,128]{2,1,0:T(8,128)}), f32[2,16,128]{2,1,0:T(8,128)S(1)}, u32[]{:S(2)}, u32[]{:S(2)}) async-start(f32[2,16,128]{2,1,0:T(8,128)} %bitcast.88), calls=%async_computation | async-start | bytes 32768 | tf_op jit(solution)/shard_map/all_to_all | solution.py:20
  233.0 544.2 %copy-start.3 = (bf16[32,16,128]{0,1,2:T(8,128)(2,1)S(1)}, bf16[32,16,128]{0,1,2:T(8,128)(2,1)}, u32[]{:S(2)}) copy-start(bf16[32,16,128]{0,1,2:T(8,128)(2,1)} %copy.35) | copy-start | bytes 393220
Sparse Core Ops, SparseCore 0:
  210.4 566.7 reduce-scatter.1
where the time goes:
time: 788 us
  waiting for transfers between devices  538 us (68%)
  blocking collectives  164 us (21%)
  matrix products  38.2 us (5%)
  local copies, waits for them, and re-layouts  17.6 us (2%)
  between operations  14.2 us (2%)
  starting transfers between devices  12.5 us (2%)
    reduce_scatter x1, waiting for transfers between devices, body(): lax.psum_scatter(grad_terms, 'curve', scatter_dimension=0, tiled=True)[0]  534 us
    all_gather x1, blocking collectives, body(): every = lax.all_gather(coarse[None], 'curve', axis=0, tiled=True)  164 us
  transfers between devices with their start and end apart: 5, of which 2 were waited for; matrix products, arithmetic and copies ran while one was open for 4% of the time, Pallas kernels for 0%

commit v1 on v0

--- a/solution.py
+++ b/solution.py
@@ -55,7 +55,9 @@
     far_mats = far_kernel[0]
     partners = far_index[0]
     one_hot = (partners[:, None] == lax.iota(jnp.int32, groups)[None, :]).astype(jnp.float32)
-    every = lax.all_gather(coarse[None], "curve", axis=0, tiled=True)
+    every = jnp.concatenate(
+        lax.all_to_all(jnp.stack([coarse[None]] * lax.axis_size("curve")), "curve", 0, 0), axis=0
+    )
     chosen = jnp.einsum("ag,grc->arc", one_hot, every.astype(jnp.float32), precision=exact)
     partial_coef = jnp.einsum("aqr,arc->qc", far_mats, chosen, precision=exact)
     mix_rows = lax.dynamic_slice_in_dim(channel_mix, chan_pos * width, width, 0)

time: 788 us -> 654 us (0.83)
  blocking collectives: 164 us -> 0 us
  starting transfers between devices: 12.5 us -> 25.7 us
  waiting for transfers between devices: 538 us -> 547 us
    all_gather x1 -> x0, blocking collectives: 164 us -> none  [body(): every = lax.all_gather(coarse[None], 'curve', axis=0, tiled=True)]
    all_to_all x0 -> x1, starting transfers between devices: none -> 14.8 us  [body(): lax.all_to_all(jnp.stack([coarse[None]] * lax.axis_size('curve')), 'curve...]
    reduce_scatter x1, waiting for transfers between devices: 534 us -> 547 us  [body(): lax.psum_scatter(grad_terms, 'curve', scatter_dimension=0, tiled=True)[0]]
  transfers between devices with their start and end apart: 5 -> 6, of which waited for: 2 -> 2; matrix products, arithmetic and copies ran while one was open for 4% -> 8% of each run, Pallas kernels for 0% -> 0%
where the time goes in v1:
time: 654 us; the launch traced here: 652 us
  waiting for transfers between devices  547 us (84%)
  matrix products  41.2 us (6%)
  starting transfers between devices  25.7 us (4%)
  local copies, waits for them, and re-layouts  20.6 us (3%)
  between operations  14.2 us (2%)
    reduce_scatter x1, waiting for transfers between devices, body(): lax.psum_scatter(grad_terms, 'curve', scatter_dimension=0, tiled=True)[0]  547 us
    all_to_all x1, starting transfers between devices, body(): lax.all_to_all(jnp.stack([coarse[None]] * lax.axis_size('curve')), 'curve...  14.8 us
  transfers between devices with their start and end apart: 6, of which 2 were waited for; matrix products, arithmetic and copies ran while one was open for 8% of the time, Pallas kernels for 0%

profile of v1, /device:TPU:0, one launch (start us, length us, event | category | flops | bytes accessed | tf_op | source)
XLA Modules:
  0.0 652.1 jit_solution(13036402640979762524)
XLA Ops:
  7.2 1.2 copy-done
  8.4 1.1 convolution_bitcast_fusion.3
  9.5 1.1 convolution_bitcast_fusion.1
  10.7 0.6 copy.68
  11.3 3.2 all-to-all-start.2
  14.5 1.4 collective-permute-start
  15.9 0.7 iota_compare_fusion.2
  16.6 0.7 compare_select_fusion
  17.3 7.9 %subtract_convert_fusion = (bf16[32,8,128,128]{3,2,1,0:T(8,128)(2,1)S(1)}, bf16[32,8,128,128]{3,2,1,0:T(8,128)(2,1)}) fusion(bf16[32,8,128,128]{3,2,1,0:T(8,128)(2,1)} %param.12, bf16[32,128,128,1]{2,1,3,0:T(8,128)(2,1)S(1)} %bitcast.91), kind=kOutput, calls=%fused_computation.1 | convolution fusion | flops 1090519040 | bytes 26214400 | tf_op jit(solution)/shard_map/bspq,bpc->bsqc/dot_general | solution.py:69
  25.2 7.0 %fusion = f32[64,128,128,1]{2,0,3,1:T(8,128)} fusion(bf16[32,8,128,128]{3,2,1,0:T(8,128)(2,1)S(1)} %get-tuple-element.2, s32[32,8]{0,1:T(8,128)S(1)} %get-tuple-element.5, pred[32,8]{0,1:T(8,128)(4,1)S(1)} %get-tuple-element.6), kind=kOutput, calls=%fused_computation.2 | convolution fusion | flops 536903680 | bytes 12584192 | tf_op jit(solution)/shard_map/bse,bsqc->eqc/dot_general | solution.py:81
  32.2 0.2 fusion.14
  32.5 0.9 stack.3
  33.4 14.8 %all-to-all-start = ((bf16[128,1,16,128]{3,2,1,0:T(8,128)(2,1)}), bf16[128,1,16,128]{3,2,1,0:T(8,128)(2,1)S(1)}, u32[]{:S(2)}, u32[]{:S(2)}) async-start(bf16[128,1,16,128]{3,2,1,0:T(8,128)(2,1)} %stack.3), calls=%async_computation | async-start | bytes 1048576 | tf_op jit(solution)/shard_map/all_to_all | solution.py:59
  48.2 0.2 reduce-scatter.2.cloned.1.call-start
  48.5 9.9 %bitcast_add_fusion = f32[64,128,128]{2,0,1:T(8,128)S(1)} fusion(f32[64,128,128,1]{2,0,3,1:T(8,128)} %fusion, bf16[32,8,128,128]{3,2,1,0:T(8,128)(2,1)} %get-tuple-element.3, s32[32,8]{0,1:T(8,128)S(1)} %get-tuple-element.5, pred[32,8]{0,1:T(8,128)(4,1)S(1)} %get-tuple-element.6), kind=kOutput, calls=%fused_computation.8 | convolution fusion | flops 537952256 | bytes 16778496 | tf_op jit(solution)/shard_map/bse,bsqc->eqc/dot_general | solution.py:78
  58.4 2.0 copy-done.1
  60.4 1.2 slice.19
  61.6 1.3 collective-permute-start.1
  63.4 0.7 fusion.35
  64.1 1.6 copy.46
  65.7 1.3 copy.47
  67.2 0.2 fusion.15
  67.9 0.6 copy.69
  68.5 4.8 all-to-all-start.1
  73.3 1.0 copy-done.4
  74.3 1.7 pad_maximum_fusion
  76.0 8.5 %gather_fusion = bf16[256,128,128]{2,1,0:T(8,128)(2,1)} fusion(bf16[64,128,128]{2,1,0:T(8,128)(2,1)S(1)} %pad_maximum_fusion, s32[1024]{0:T(1024)S(1)} %pad_clamp_fusion), kind=kCustom, calls=%fused_computation | custom fusion | bytes 16778240 | tf_op jit(solution)/shard_map/gather | solution.py:52
  84.6 0.5 fusion.30
  85.1 9.3 %fusion.11 = bf16[32,128,128]{2,1,0:T(8,128)(2,1)} fusion(f32[128,32,128]{0,2,1:T(8,128)S(1)} %fusion.30, bf16[32,8,128,128]{3,2,1,0:T(8,128)(2,1)} %param.12, bf16[32,8,128,128]{3,2,1,0:T(8,128)(2,1)} %bitcast.93, bf16[32,8]{1,0:T(8,128)(2,1)S(1)} %copy.37), kind=kOutput, calls=%fused_computation.16 | convolution fusion | flops 1091567616 | bytes 19923456 | tf_op jit(solution)/shard_map/bspq,bsqc->bpc/dot_general | solution.py:53
  94.4 547.0 %reduce-scatter.2.cloned.1.call-done = f32[1,16,128]{2,1,0:T(8,128)} async-done(((f32[128,16,128]{2,1,0:T(8,128)}), f32[1,16,128]{2,1,0:T(8,128)}) %reduce-scatter.2.cloned.1.call-update) | async-done | bytes 8208 | tf_op jit(solution)/shard_map/reduce_scatter | solution.py:90
  641.5 2.4 fusion.10
  643.9 1.4 copy.48
  (33 shorter events, 1.2 us)
Async XLA Ops:
  7.2 1.2 copy-start
  11.3 21.2 %all-to-all-start.2 = ((f32[2,16,128]{2,1,0:T(8,128)}), f32[2,16,128]{2,1,0:T(8,128)S(1)}, u32[]{:S(2)}, u32[]{:S(2)}) async-start(f32[2,16,128]{2,1,0:T(8,128)} %bitcast.88), calls=%async_computation.2 | async-start | bytes 32768 | tf_op jit(solution)/shard_map/all_to_all | solution.py:20
  14.5 58.8 %collective-permute-start = (bf16[4096,128]{1,0:T(8,128)(2,1)}, bf16[4096,128]{1,0:T(8,128)(2,1)S(1)}, u32[]{:S(2)}, u32[]{:S(2)}) collective-permute-start(bf16[4096,128]{1,0:T(8,128)(2,1)} %param.10), channel_id=1, source_target_pairs={{0,2},{2,4},{4,6},{6,8},{8,10},{10,12},{12,14},{14,16},{16,18},{18... | collective-permute-start | bytes 3145736 | tf_op jit(solution)/shard_map/ppermute | solution.py:10
  25.2 7.1 %copy-start.2 = (bf16[4096,128]{1,0:T(8,128)(2,1)S(1)}, bf16[4096,128]{1,0:T(8,128)(2,1)}, u32[]{:S(2)}) copy-start(bf16[4096,128]{1,0:T(8,128)(2,1)} %param.10) | copy-start | bytes 3145732
  25.2 7.1 %copy-start.5 = (bf16[32,16,128]{2,1,0:T(8,128)(2,1)S(1)}, bf16[32,16,128]{2,1,0:T(8,128)(2,1)}, u32[]{:S(2)}) copy-start(bf16[32,16,128]{2,1,0:T(8,128)(2,1)} %param.15) | copy-start | bytes 393220
  33.4 33.9 %all-to-all-start = ((bf16[128,1,16,128]{3,2,1,0:T(8,128)(2,1)}), bf16[128,1,16,128]{3,2,1,0:T(8,128)(2,1)S(1)}, u32[]{:S(2)}, u32[]{:S(2)}) async-start(bf16[128,1,16,128]{3,2,1,0:T(8,128)(2,1)} %stack.3), calls=%async_computation | async-start | bytes 1048576 | tf_op jit(solution)/shard_map/all_to_all | solution.py:59
  48.2 593.2 %reduce-scatter.2.cloned.1.call-start = ((), (), s32[]{:S(2)}) async-start(), calls=%async_computation.4 | async-start | bytes 1056768 | tf_op jit(solution)/shard_map/reduce_scatter | solution.py:90
  48.4 14.5 %copy-start.8 = (f32[1,8,16,16]{3,2,1,0:T(8,128)S(1)}, f32[1,8,16,16]{3,2,1,0:T(8,128)}, u32[]{:S(2)}) copy-start(f32[1,8,16,16]{3,2,1,0:T(8,128)} %param.17) | copy-start | bytes 24580
  48.5 14.9 %copy-start.9 = (s32[1,8]{1,0:T(1,128)S(1)}, s32[1,8]{1,0:T(1,128)}, u32[]{:S(2)}) copy-start(s32[1,8]{1,0:T(1,128)} %param.18) | copy-start | bytes 100
  48.5 19.2 %copy-start.7 = (f32[256,256]{1,0:T(8,128)S(1)}, f32[256,256]{1,0:T(8,128)}, u32[]{:S(2)}) copy-start(f32[256,256]{1,0:T(8,128)} %param.19) | copy-start | bytes 786436
  58.4 2.0 copy-start.1
  61.6 32.8 %collective-permute-start.1 = (bf16[32,128,128]{2,0,1:T(8,128)(2,1)}, bf16[32,128,128]{2,0,1:T(8,128)(2,1)}, u32[]{:S(2)}, u32[]{:S(2)}) collective-permute-start(bf16[32,128,128]{2,0,1:T(8,128)(2,1)} %slice.19), channel_id=1, source_target_pairs={{2,0},{4,2},{6,4},{8,6},{10,8},{12,10},{14,12},{16,14},{18,16},{20... | collective-permute-start | bytes 3145736 | tf_op jit(solution)/shard_map/ppermute | solution.py:10
  68.5 16.0 %all-to-all-start.1 = ((f32[2,16,128]{2,1,0:T(8,128)}), f32[2,16,128]{2,1,0:T(8,128)S(1)}, u32[]{:S(2)}, u32[]{:S(2)}) async-start(f32[2,16,128]{2,1,0:T(8,128)} %bitcast.90), calls=%async_computation.1 | async-start | bytes 32768 | tf_op jit(solution)/shard_map/all_to_all | solution.py:20
  73.3 1.0 copy-start.4
  76.0 8.5 %copy-start.6 = (bf16[32,128,16]{1,2,0:T(8,128)(2,1)S(1)}, bf16[32,128,16]{1,2,0:T(8,128)(2,1)}, u32[]{:S(2)}) copy-start(bf16[32,128,16]{1,2,0:T(8,128)(2,1)} %param.16) | copy-start | bytes 393220
  85.1 556.4 %copy-start.3 = (bf16[32,16,128]{0,1,2:T(8,128)(2,1)S(1)}, bf16[32,16,128]{0,1,2:T(8,128)(2,1)}, u32[]{:S(2)}) copy-start(bf16[32,16,128]{0,1,2:T(8,128)(2,1)} %copy.47) | copy-start | bytes 393220
Sparse Core Ops, SparseCore 0:
  65.8 575.5 reduce-scatter.1
